TPU v7x, 32 devices: a whole 2x2x4 slice. The times are simulated.
32 devices in a mesh: gx: 4 (over x, core), gy: 2 (over y), orb: 4 (over z).
Axes of the slice: x: 2, y: 2, z: 4, core: 2. Of those that a mesh axis runs over, the one named last changes fastest.
Arguments:
- orbitals: float32 [4, 32, 32, 384], P('orb', 'gx', 'gy'), may hold values from -6 to 6
- local_pot: float32 [32, 32, 384], P('gx', 'gy'), may hold values from -1 to 1
- proj_vals: bfloat16 [4, 32, 32, 384], P(None, 'gx', 'gy'), may hold values from -0.29882812 to 0.29882812
- proj_ids: int32 [4, 32, 32, 3], P(None, 'gx', 'gy'), may hold values from 0 to 4095, as said below
- proj_energy: float32 [4096], replicated, may hold values from 0.5 to 2
- cheb_coef: float32 [4], replicated, may hold values from 0.2 to 1
Outputs:
- density: float32 [32, 32, 384], P('gx', 'gy')
Inputs may be any that keep to these rules, and one draw needn't show every extreme that they name: `proj_ids`: the owner o = id // 512 of each id names the column block (o // 2, o % 2); it differs from the block (x // 8, y // 16) of the slot's cells by at most one in each of the two coordinates, periodically.
All inputs are finite; a program needn't handle non-finite values.
Results may differ from a plain program's by a relative error of at most 0.0003.
Values sent between devices are 32-bit elements; how exact they have to be, the bound alone decides.
No kernel may reach another device: no remote copies, remote signals or barrier semaphores. Data moves between devices by JAX's collectives and lax.ppermute only.
A program may use at most 64 MiB of HBM per device.

v0:
```python
import jax
import jax.numpy as jnp
from jax import lax
from jax.sharding import PartitionSpec as P

ZB = 128
STEPS = 3
E_MID = 4.0
E_HALF = 8.0
PRECISE = lax.Precision.HIGHEST


def extended(block, sides, width):
    for axis, dim in sides:
        count = lax.axis_size(axis)
        forward = [(i, i + 1) for i in range(count - 1)]
        forward.append((count - 1, 0))
        backward = [(target, source) for source, target in forward]
        low = lax.ppermute(
            lax.slice_in_dim(block, block.shape[dim] - width, None, axis=dim), axis, forward
        )
        high = lax.ppermute(lax.slice_in_dim(block, 0, width, axis=dim), axis, backward)
        block = jnp.concatenate([low, block, high], axis=dim)
    return block


def stencil(grid_vals):
    extent_first = grid_vals.shape[1]
    extent_second = grid_vals.shape[2]
    padded = extended(grid_vals, (("gx", 1), ("gy", 2)), 2)
    middle_rows = padded[:, :, 2 : 2 + extent_second]
    middle_cols = padded[:, 2 : 2 + extent_first]
    result = -90.0 * grid_vals
    result = (
        result
        + 16.0 * (middle_rows[:, 1 : 1 + extent_first] + middle_rows[:, 3 : 3 + extent_first])
        - (middle_rows[:, 0:extent_first] + middle_rows[:, 4 : 4 + extent_first])
    )
    result = (
        result
        + 16.0
        * (middle_cols[:, :, 1 : 1 + extent_second] + middle_cols[:, :, 3 : 3 + extent_second])
        - (middle_cols[:, :, 0:extent_second] + middle_cols[:, :, 4 : 4 + extent_second])
    )
    result = (
        result
        + 16.0 * (jnp.roll(grid_vals, 1, 3) + jnp.roll(grid_vals, -1, 3))
        - (jnp.roll(grid_vals, 2, 3) + jnp.roll(grid_vals, -2, 3))
    )
    return result / 12.0


def local(orbitals, local_pot, proj_vals, proj_ids, proj_energy, cheb_coef):
    count_orb = orbitals.shape[0]
    extent_first = orbitals.shape[1]
    extent_second = orbitals.shape[2]
    extent_depth = orbitals.shape[3]
    slot_count = proj_vals.shape[0]
    block_count = extent_depth // ZB
    count_all = proj_energy.shape[0]
    shaped = proj_vals.astype(jnp.float32).reshape(
        slot_count, extent_first, extent_second, block_count, ZB
    )
    ids_flat = proj_ids.reshape(-1)

    def weights_of(blocks):
        partial_value = jax.vmap(
            lambda single: jax.ops.segment_sum(single, ids_flat, num_segments=count_all)
        )(blocks.reshape(count_orb, -1))
        coef_sums = lax.psum(partial_value, ("gx", "gy"))
        return jnp.take(coef_sums * proj_energy[None, :], ids_flat, axis=1)

    def hamilton(grid_vals):
        blocks = jnp.einsum(
            "kxyzb,oxyzb->okxyz",
            shaped,
            grid_vals.reshape(count_orb, extent_first, extent_second, block_count, ZB),
            precision=PRECISE,
        )
        weights = weights_of(blocks).reshape(
            count_orb, slot_count, extent_first, extent_second, block_count
        )
        projected = jnp.einsum("kxyzb,okxyz->oxyzb", shaped, weights, precision=PRECISE).reshape(
            grid_vals.shape
        )
        return (
            -0.5 * stencil(grid_vals) + local_pot[None] * grid_vals + projected - E_MID * grid_vals
        ) / E_HALF

    previous = orbitals
    current = hamilton(orbitals)
    filtered = cheb_coef[0] * previous + cheb_coef[1] * current
    for degree in range(2, STEPS + 1):
        following = 2.0 * hamilton(current) - previous
        previous = current
        current = following
        filtered = filtered + cheb_coef[degree] * current
    density = lax.psum(jnp.sum(filtered * filtered, axis=0), "orb")
    return density / (count_orb * lax.axis_size("orb"))


def solution(mesh):
    return jax.shard_map(
        local,
        mesh=mesh,
        in_specs=(
            P("orb", "gx", "gy", None),
            P("gx", "gy", None),
            P(None, "gx", "gy", None),
            P(None, "gx", "gy", None),
            P(),
            P(),
        ),
        out_specs=P("gx", "gy", None),
        check_vma=False,
    )
```

profile of v0, /device:TPU:0, one launch (start us, length us, event | category | flops | bytes accessed | tf_op | source)
XLA Modules:
  0.0 220.9 jit_solution(10837765373750434986)
XLA Ops:
  7.9 2.0 collective-permute-start.1
  11.9 1.4 fusion.78
  15.6 8.6 %scatter_custom_fusion = f32[4096]{0:T(1024)S(1)} fusion(s32[1536]{0:T(1024)S(1)} %reshape.438, f32[1536]{0:T(1024)S(1)} %reshape.440, f32[]{:T(128)} %constant.38.clone.1), kind=kCustom, calls=%fused_computation.125 | custom fusion | flops 1536 | bytes 16388 | tf_op jit(solution)/shard_map/vmap()/scatter-add | solution.py:68
  24.2 24.7 %psum.28 = f32[1,4096]{1,0:T(1,128)S(1)} all-reduce(f32[1,4096]{1,0:T(1,128)S(1)} %bitcast.82), channel_id=1, replica_groups=mesh['gx'=4,'gy'=2,'orb'=4] {'gx','gy'}, use_global_device_ids=true, to_apply=%region_1.0 | all-reduce | flops 4096 | bytes 32768 | tf_op jit(solution)/shard_map/psum | solution.py:70
  49.6 8.4 %gather_fusion = f32[1536]{0:T(1024)S(1)} fusion(f32[4096]{0:T(1024)S(1)} %bitcast.70, s32[2048]{0:T(1024)S(1)} %pad_clamp_fusion), kind=kCustom, calls=%fused_computation.clone | custom fusion | bytes 18432 | tf_op jit(solution)/shard_map/jit(_take)/gather | solution.py:71
  59.1 1.4 fusion.79
  60.9 2.0 collective-permute-start.3
  67.4 1.7 collective-permute-start.5
  69.2 1.4 fusion.80
  71.8 8.6 %scatter_custom_fusion.1 = f32[4096]{0:T(1024)S(1)} fusion(s32[1536]{0:T(1024)S(1)} %reshape.438, f32[1536]{0:T(1024)S(1)} %reshape.450, f32[]{:T(128)} %constant.38.clone.1), kind=kCustom, calls=%fused_computation.123 | custom fusion | flops 1536 | bytes 16388 | tf_op jit(solution)/shard_map/vmap()/scatter-add | solution.py:68
  80.4 24.0 %psum.29 = f32[1,4096]{1,0:T(1,128)S(1)} all-reduce(f32[1,4096]{1,0:T(1,128)S(1)} %bitcast.83), channel_id=1, replica_groups=mesh['gx'=4,'gy'=2,'orb'=4] {'gx','gy'}, use_global_device_ids=true, to_apply=%region_3.5 | all-reduce | flops 4096 | bytes 32768 | tf_op jit(solution)/shard_map/psum | solution.py:70
  104.4 8.4 %gather_fusion.1 = f32[1536]{0:T(1024)S(1)} fusion(f32[4096]{0:T(1024)S(1)} %bitcast.71, s32[2048]{0:T(1024)S(1)} %pad_clamp_fusion), kind=kCustom, calls=%fused_computation.1.clone | custom fusion | bytes 18432 | tf_op jit(solution)/shard_map/jit(_take)/gather | solution.py:71
  113.9 1.4 fusion.81
  116.1 1.4 collective-permute-start.7
  117.8 1.7 collective-permute-done.6
  120.9 1.7 collective-permute-start.9
  125.3 8.6 %scatter_custom_fusion.2 = f32[4096]{0:T(1024)S(1)} fusion(s32[1536]{0:T(1024)S(1)} %reshape.438, f32[1536]{0:T(1024)S(1)} %reshape.460, f32[]{:T(128)} %constant.38.clone.1), kind=kCustom, calls=%fused_computation.121 | custom fusion | flops 1536 | bytes 16388 | tf_op jit(solution)/shard_map/vmap()/scatter-add | solution.py:68
  133.9 23.8 %psum.30 = f32[1,4096]{1,0:T(1,128)S(1)} all-reduce(f32[1,4096]{1,0:T(1,128)S(1)} %bitcast.81), channel_id=1, replica_groups=mesh['gx'=4,'gy'=2,'orb'=4] {'gx','gy'}, use_global_device_ids=true, to_apply=%region_5.7 | all-reduce | flops 4096 | bytes 32768 | tf_op jit(solution)/shard_map/psum | solution.py:70
  157.7 8.4 %gather_fusion.2 = f32[1536]{0:T(1024)S(1)} fusion(f32[4096]{0:T(1024)S(1)} %bitcast.69, s32[2048]{0:T(1024)S(1)} %pad_clamp_fusion), kind=kCustom, calls=%fused_computation.2.clone | custom fusion | bytes 18432 | tf_op jit(solution)/shard_map/jit(_take)/gather | solution.py:71
  167.2 1.4 fusion.83
  171.1 1.7 collective-permute-done.10
  173.6 3.0 %multiply_bitcast_fusion = f32[8,16,384]{2,1,0:T(8,128)} fusion(f32[1,8,16,384]{3,2,1,0:T(8,128)S(1)} %fusion.30, f32[1,8,16,384]{3,2,1,0:T(8,128)S(1)} %get-tuple-element.7, f32[1,8,16,384]{3,2,1,0:T(8,128)S(1)} %copy-done, f32[1,8,16,384]{3,2,1,0:T(8,128)S(1)} %transpose.23, f32[8,16,384]{2,1,0:T(8,128)S(1)} %copy-done.1, ...), kind=kLoop, calls=%fused_computation.103 | loop fusion | flops 2605056 | bytes 2138128 | tf_op jit(solution)/shard_map/reduce_sum | solution.py:98
  176.6 35.8 %all-reduce.2.cloned.1.call-done = f32[8,16,384]{2,1,0:T(8,128)} async-done(((f32[8,16,384]{2,1,0:T(8,128)}), f32[8,16,384]{2,1,0:T(8,128)}) %all-reduce.2.cloned.1.call-update) | async-done | bytes 196624 | tf_op jit(solution)/shard_map/psum | solution.py:98
  212.4 1.6 broadcast_multiply_fusion
  (91 shorter events, 23.4 us)
Async XLA Ops:
  6.5 3.4 %copy-start = (f32[1,8,16,384]{3,2,1,0:T(8,128)S(1)}, f32[1,8,16,384]{3,2,1,0:T(8,128)}, u32[]{:S(2)}) copy-start(f32[1,8,16,384]{3,2,1,0:T(8,128)} %param.8) | copy-start | bytes 589828
  6.5 205.9 %all-reduce.2.cloned.1.call-start = ((), (), s32[]{:S(2)}) async-start(), calls=%async_computation | async-start | bytes 393216 | tf_op jit(solution)/shard_map/psum | solution.py:98
  7.4 53.2 %collective-permute-start = (f32[1,2,16,384]{3,2,1,0:T(8,128)S(1)}, f32[1,2,16,384]{3,2,1,0:T(8,128)S(1)}, u32[]{:S(2)}, u32[]{:S(2)}) collective-permute-start(f32[1,2,16,384]{3,2,1,0:T(8,128)S(1)} %get-tuple-element.40), channel_id=1, source_target_pairs={{0,8},{8,16},{16,24},{24,0},{1,9},{9,17},{17,25},{25,1},{2,10},{10... | collective-permute-start | bytes 147464 | tf_op jit(solution)/shard_map/ppermute | solution.py:19
  7.9 52.8 %collective-permute-start.1 = (f32[1,2,16,384]{3,2,1,0:T(8,128)S(1)}, f32[1,2,16,384]{3,2,1,0:T(8,128)S(1)}, u32[]{:S(2)}, u32[]{:S(2)}) collective-permute-start(f32[1,2,16,384]{3,2,1,0:T(8,128)S(1)} %get-tuple-element.39), channel_id=1, source_target_pairs={{8,0},{16,8},{24,16},{0,24},{9,1},{17,9},{25,17},{1,25},{10,2},{18... | collective-permute-start | bytes 147464 | tf_op jit(solution)/shard_map/ppermute | solution.py:22
  10.2 1.0 copy-start.2
  14.3 0.8 copy-start.4
  48.9 0.7 copy-start.3
  60.7 2.1 copy-start.6
  60.7 4.0 %collective-permute-start.2 = (f32[1,12,2,384]{3,2,1,0:T(2,128)S(1)}, f32[1,12,2,384]{3,2,1,0:T(2,128)S(1)}, u32[]{:S(2)}, u32[]{:S(2)}) collective-permute-start(f32[1,12,2,384]{3,2,1,0:T(2,128)S(1)} %get-tuple-element.14), channel_id=1, source_target_pairs={{0,4},{4,0},{1,5},{5,1},{2,6},{6,2},{3,7},{7,3},{8,12},{12,8},{9,1... | collective-permute-start | bytes 110600 | tf_op jit(solution)/shard_map/ppermute | solution.py:19
  60.9 4.3 %collective-permute-start.3 = (f32[1,12,2,384]{3,2,1,0:T(2,128)S(1)}, f32[1,12,2,384]{3,2,1,0:T(2,128)S(1)}, u32[]{:S(2)}, u32[]{:S(2)}) collective-permute-start(f32[1,12,2,384]{3,2,1,0:T(2,128)S(1)} %get-tuple-element.15), channel_id=1, source_target_pairs={{4,0},{0,4},{5,1},{1,5},{6,2},{2,6},{7,3},{3,7},{12,8},{8,12},{13,... | collective-permute-start | bytes 110600 | tf_op jit(solution)/shard_map/ppermute | solution.py:22
  63.5 2.2 %copy-start.1 = (f32[8,16,384]{2,1,0:T(8,128)S(1)}, f32[8,16,384]{2,1,0:T(8,128)}, u32[]{:S(2)}) copy-start(f32[8,16,384]{2,1,0:T(8,128)} %param.9) | copy-start | bytes 589828
  65.2 0.6 copy-start.5
  67.4 48.1 %collective-permute-start.4 = (f32[1,2,16,384]{3,2,1,0:T(8,128)S(1)}, f32[1,2,16,384]{3,2,1,0:T(8,128)S(1)}, u32[]{:S(2)}, u32[]{:S(2)}) collective-permute-start(f32[1,2,16,384]{3,2,1,0:T(8,128)S(1)} %get-tuple-element.34), channel_id=1, source_target_pairs={{0,8},{8,16},{16,24},{24,0},{1,9},{9,17},{17,25},{25,1},{2,10},{10... | collective-permute-start | bytes 147464 | tf_op jit(solution)/shard_map/ppermute | solution.py:19
  67.4 48.0 %collective-permute-start.5 = (f32[1,2,16,384]{3,2,1,0:T(8,128)S(1)}, f32[1,2,16,384]{3,2,1,0:T(8,128)S(1)}, u32[]{:S(2)}, u32[]{:S(2)}) collective-permute-start(f32[1,2,16,384]{3,2,1,0:T(8,128)S(1)} %get-tuple-element.35), channel_id=1, source_target_pairs={{8,0},{16,8},{24,16},{0,24},{9,1},{17,9},{25,17},{1,25},{10,2},{18... | collective-permute-start | bytes 147464 | tf_op jit(solution)/shard_map/ppermute | solution.py:22
  115.5 4.0 %collective-permute-start.6 = (f32[1,12,2,384]{3,2,1,0:T(2,128)S(1)}, f32[1,12,2,384]{3,2,1,0:T(2,128)S(1)}, u32[]{:S(2)}, u32[]{:S(2)}) collective-permute-start(f32[1,12,2,384]{3,2,1,0:T(2,128)S(1)} %get-tuple-element.12), channel_id=1, source_target_pairs={{0,4},{4,0},{1,5},{5,1},{2,6},{6,2},{3,7},{7,3},{8,12},{12,8},{9,1... | collective-permute-start | bytes 110600 | tf_op jit(solution)/shard_map/ppermute | solution.py:19
  116.1 4.0 %collective-permute-start.7 = (f32[1,12,2,384]{3,2,1,0:T(2,128)S(1)}, f32[1,12,2,384]{3,2,1,0:T(2,128)S(1)}, u32[]{:S(2)}, u32[]{:S(2)}) collective-permute-start(f32[1,12,2,384]{3,2,1,0:T(2,128)S(1)} %get-tuple-element.13), channel_id=1, source_target_pairs={{4,0},{0,4},{5,1},{1,5},{6,2},{2,6},{7,3},{3,7},{12,8},{8,12},{13,... | collective-permute-start | bytes 110600 | tf_op jit(solution)/shard_map/ppermute | solution.py:22
  120.9 47.8 %collective-permute-start.8 = (f32[1,2,16,384]{3,2,1,0:T(8,128)S(1)}, f32[1,2,16,384]{3,2,1,0:T(8,128)S(1)}, u32[]{:S(2)}, u32[]{:S(2)}) collective-permute-start(f32[1,2,16,384]{3,2,1,0:T(8,128)S(1)} %get-tuple-element.16), channel_id=1, source_target_pairs={{0,8},{8,16},{16,24},{24,0},{1,9},{9,17},{17,25},{25,1},{2,10},{10... | collective-permute-start | bytes 147464 | tf_op jit(solution)/shard_map/ppermute | solution.py:19
  120.9 47.8 %collective-permute-start.9 = (f32[1,2,16,384]{3,2,1,0:T(8,128)S(1)}, f32[1,2,16,384]{3,2,1,0:T(8,128)S(1)}, u32[]{:S(2)}, u32[]{:S(2)}) collective-permute-start(f32[1,2,16,384]{3,2,1,0:T(8,128)S(1)} %get-tuple-element.17), channel_id=1, source_target_pairs={{8,0},{16,8},{24,16},{0,24},{9,1},{17,9},{25,17},{1,25},{10,2},{18... | collective-permute-start | bytes 147464 | tf_op jit(solution)/shard_map/ppermute | solution.py:22
  168.7 4.0 %collective-permute-start.10 = (f32[1,12,2,384]{3,2,1,0:T(2,128)S(1)}, f32[1,12,2,384]{3,2,1,0:T(2,128)S(1)}, u32[]{:S(2)}, u32[]{:S(2)}) collective-permute-start(f32[1,12,2,384]{3,2,1,0:T(2,128)S(1)} %get-tuple-element.10), channel_id=1, source_target_pairs={{0,4},{4,0},{1,5},{5,1},{2,6},{6,2},{3,7},{7,3},{8,12},{12,8},{9,1... | collective-permute-start | bytes 110600 | tf_op jit(solution)/shard_map/ppermute | solution.py:19
  169.6 4.0 %collective-permute-start.11 = (f32[1,12,2,384]{3,2,1,0:T(2,128)S(1)}, f32[1,12,2,384]{3,2,1,0:T(2,128)S(1)}, u32[]{:S(2)}, u32[]{:S(2)}) collective-permute-start(f32[1,12,2,384]{3,2,1,0:T(2,128)S(1)} %get-tuple-element.11), channel_id=1, source_target_pairs={{4,0},{0,4},{5,1},{1,5},{6,2},{2,6},{7,3},{3,7},{12,8},{8,12},{13,... | collective-permute-start | bytes 110600 | tf_op jit(solution)/shard_map/ppermute | solution.py:22
Sparse Core Ops, SparseCore 0:
  176.7 35.6 all-reduce.1
where the time goes:
time: 221 us
  blocking collectives  72.5 us (33%)
  waiting for transfers between devices  41.5 us (19%)
  local copies, waits for them, and re-layouts  39.7 us (18%)
  other arithmetic  31.9 us (14%)
  between operations  14.5 us (7%)
  starting transfers between devices  12.3 us (6%)
  matrix products  8.32 us (4%)
    psum x3, blocking collectives, weights_of(): coef_sums = lax.psum(partial_value, ('gx', 'gy'))  72.5 us
    psum x1, waiting for transfers between devices, local(): density = lax.psum(jnp.sum(filtered * filtered, axis=0), 'orb')  35.8 us
    scatter-add x3, other arithmetic, weights_of(): jax.ops.segment_sum(single, ids_flat, num_segments=count_all)  25.8 us
    gather x3, local copies, waits for them, and re-layouts, weights_of(): return jnp.take(coef_sums * proj_energy[None, :], ids_flat, axis=1)  25.2 us
    ppermute x6, starting transfers between devices, extended(): lax.ppermute(lax.slice_in_dim(block, 0, width, axis=dim), axis, backward)  10 us
  transfers between devices with their start and end apart: 13, of which 7 were waited for; matrix products, arithmetic and copies ran while one was open for 31% of the time, Pallas kernels for 0%

commit v1 on v0

--- a/solution.py
+++ b/solution.py
@@ -67,7 +67,7 @@
         partial_value = jax.vmap(
             lambda single: jax.ops.segment_sum(single, ids_flat, num_segments=count_all)
         )(blocks.reshape(count_orb, -1))
-        coef_sums = lax.psum(partial_value, ("gx", "gy"))
+        coef_sums = jnp.sum(lax.all_gather(partial_value, axis_name=("gx", "gy")), 0)
         return jnp.take(coef_sums * proj_energy[None, :], ids_flat, axis=1)
 
     def hamilton(grid_vals):

time: 221 us -> 199 us (0.900)
  blocking collectives: 72.5 us -> 49.8 us
    psum x3 -> x0, blocking collectives: 72.5 us -> none  [weights_of(): coef_sums = lax.psum(partial_value, ('gx', 'gy'))]
    all_gather x0 -> x3, blocking collectives: none -> 49.8 us  [weights_of(): lax.all_gather(partial_value, axis_name=('gx', 'gy'))]
  transfers between devices with their start and end apart: 13 -> 13, of which waited for: 7 -> 7; matrix products, arithmetic and copies ran while one was open for 31% -> 35% of each run, Pallas kernels for 0% -> 0%
where the time goes in v1:
time: 199 us; the launch traced here: 198 us
  blocking collectives  49.8 us (25%)
  waiting for transfers between devices  41.5 us (21%)
  local copies, waits for them, and re-layouts  39.8 us (20%)
  other arithmetic  32 us (16%)
  between operations  14.6 us (7%)
  starting transfers between devices  12.3 us (6%)
  matrix products  8.32 us (4%)
    all_gather x3, blocking collectives, weights_of(): lax.all_gather(partial_value, axis_name=('gx', 'gy'))  49.8 us
    psum x1, waiting for transfers between devices, local(): density = lax.psum(jnp.sum(filtered * filtered, axis=0), 'orb')  35.4 us
    scatter-add x3, other arithmetic, weights_of(): jax.ops.segment_sum(single, ids_flat, num_segments=count_all)  25.8 us
    gather x3, local copies, waits for them, and re-layouts, weights_of(): return jnp.take(coef_sums * proj_energy[None, :], ids_flat, axis=1)  25.2 us
    ppermute x6, starting transfers between devices, extended(): lax.ppermute(lax.slice_in_dim(block, 0, width, axis=dim), axis, backward)  10.4 us
    ppermute x6, waiting for transfers between devices, extended(): lax.ppermute(lax.slice_in_dim(block, block.shape[dim] - width, None, axis...  4.57 us
    dot_general x3, matrix products, hamilton(): jnp.einsum('kxyzb,okxyz->oxyzb', shaped, weights, precision=PRECISE)  4.19 us
    dot_general x3, matrix products, hamilton(): jnp.einsum('kxyzb,oxyzb->okxyz', shaped, grid_vals.reshape(count_orb, ext...  4.12 us
  transfers between devices with their start and end apart: 13, of which 7 were waited for; matrix products, arithmetic and copies ran while one was open for 35% of the time, Pallas kernels for 0%

profile of v1, /device:TPU:0, one launch (start us, length us, event | category | flops | bytes accessed | tf_op | source)
XLA Modules:
  0.0 198.3 jit_solution(8921005641796184764)
XLA Ops:
  7.9 2.0 %collective-permute-start.1 = (f32[1,2,16,384]{3,2,1,0:T(8,128)S(1)}, f32[1,2,16,384]{3,2,1,0:T(8,128)S(1)}, u32[]{:S(2)}, u32[]{:S(2)}) collective-permute-start(f32[1,2,16,384]{3,2,1,0:T(8,128)S(1)} %get-tuple-element.39), channel_id=1, source_target_pairs={{8,0},{16,8},{24,16},{0,24},{9,1},{17,9},{25,17},{1,25},{10,2},{18... | collective-permute-start | bytes 147464 | tf_op jit(solution)/shard_map/ppermute | solution.py:22
  11.9 1.4 fusion.78
  15.6 8.6 %scatter_custom_fusion = f32[4096]{0:T(1024)S(1)} fusion(s32[1536]{0:T(1024)S(1)} %reshape.450, f32[1536]{0:T(1024)S(1)} %reshape.452, f32[]{:T(128)} %constant.38.clone.1), kind=kCustom, calls=%fused_computation.125 | custom fusion | flops 1536 | bytes 16388 | tf_op jit(solution)/shard_map/vmap()/scatter-add | solution.py:68
  24.2 17.2 %all-gather = f32[32768]{0:T(1024)S(1)} all-gather(f32[4096]{0:T(1024)S(1)} %scatter_custom_fusion), channel_id=2, replica_groups=mesh['gx'=4,'gy'=2,'orb'=4] {'gx','gy'}, dimensions={0}, use_global_device_ids=true | all-gather | bytes 147456 | tf_op jit(solution)/shard_map/all_gather | solution.py:70
  42.2 8.4 %gather_fusion = f32[1536]{0:T(1024)S(1)} fusion(f32[4096]{0:T(1024)S(1)} %mul.159, s32[2048]{0:T(1024)S(1)} %pad_clamp_fusion), kind=kCustom, calls=%fused_computation.clone | custom fusion | bytes 18432 | tf_op jit(solution)/shard_map/jit(_take)/gather | solution.py:71
  51.7 1.4 fusion.79
  53.8 1.6 collective-permute-start.3
  60.4 1.7 collective-permute-start.5
  64.7 8.6 %scatter_custom_fusion.1 = f32[4096]{0:T(1024)S(1)} fusion(s32[1536]{0:T(1024)S(1)} %reshape.450, f32[1536]{0:T(1024)S(1)} %reshape.462, f32[]{:T(128)} %constant.38.clone.1), kind=kCustom, calls=%fused_computation.123 | custom fusion | flops 1536 | bytes 16388 | tf_op jit(solution)/shard_map/vmap()/scatter-add | solution.py:68
  73.3 16.2 %all-gather.1 = f32[32768]{0:T(1024)S(1)} all-gather(f32[4096]{0:T(1024)S(1)} %scatter_custom_fusion.1), channel_id=3, replica_groups=mesh['gx'=4,'gy'=2,'orb'=4] {'gx','gy'}, dimensions={0}, use_global_device_ids=true | all-gather | bytes 147456 | tf_op jit(solution)/shard_map/all_gather | solution.py:70
  89.6 8.4 %gather_fusion.1 = f32[1536]{0:T(1024)S(1)} fusion(f32[4096]{0:T(1024)S(1)} %mul.174, s32[2048]{0:T(1024)S(1)} %pad_clamp_fusion), kind=kCustom, calls=%fused_computation.1.clone | custom fusion | bytes 18432 | tf_op jit(solution)/shard_map/jit(_take)/gather | solution.py:71
  99.1 1.4 fusion.81
  101.1 1.7 collective-permute-start.7
  103.0 2.1 %collective-permute-done.6 = f32[1,12,2,384]{3,2,1,0:T(2,128)S(1)} collective-permute-done((f32[1,12,2,384]{3,2,1,0:T(2,128)S(1)}, f32[1,12,2,384]{3,2,1,0:T(2,128)S(1)}, u32[]{:S(2)}, u32[]{:S(2)}) %collective-permute-start.6) | collective-permute-done | bytes 36896 | tf_op jit(solution)/shard_map/ppermute | solution.py:19
  106.3 1.7 collective-permute-start.9
  110.7 8.6 %scatter_custom_fusion.2 = f32[4096]{0:T(1024)S(1)} fusion(s32[1536]{0:T(1024)S(1)} %reshape.450, f32[1536]{0:T(1024)S(1)} %reshape.472, f32[]{:T(128)} %constant.38.clone.1), kind=kCustom, calls=%fused_computation.121 | custom fusion | flops 1536 | bytes 16388 | tf_op jit(solution)/shard_map/vmap()/scatter-add | solution.py:68
  119.3 16.4 %all-gather.2 = f32[32768]{0:T(1024)S(1)} all-gather(f32[4096]{0:T(1024)S(1)} %scatter_custom_fusion.2), channel_id=4, replica_groups=mesh['gx'=4,'gy'=2,'orb'=4] {'gx','gy'}, dimensions={0}, use_global_device_ids=true | all-gather | bytes 147456 | tf_op jit(solution)/shard_map/all_gather | solution.py:70
  135.7 8.4 %gather_fusion.2 = f32[1536]{0:T(1024)S(1)} fusion(f32[4096]{0:T(1024)S(1)} %mul.188, s32[2048]{0:T(1024)S(1)} %pad_clamp_fusion), kind=kCustom, calls=%fused_computation.2.clone | custom fusion | bytes 18432 | tf_op jit(solution)/shard_map/jit(_take)/gather | solution.py:71
  145.2 1.4 fusion.83
  147.3 1.6 collective-permute-start.11
  149.1 1.9 collective-permute-done.10
  151.5 3.0 %multiply_bitcast_fusion = f32[8,16,384]{2,1,0:T(8,128)} fusion(f32[1,8,16,384]{3,2,1,0:T(8,128)S(1)} %fusion.30, f32[1,8,16,384]{3,2,1,0:T(8,128)S(1)} %get-tuple-element.7, f32[1,8,16,384]{3,2,1,0:T(8,128)S(1)} %copy-done, f32[1,8,16,384]{3,2,1,0:T(8,128)S(1)} %transpose.23, f32[8,16,384]{2,1,0:T(8,128)S(1)} %copy-done.1, ...), kind=kLoop, calls=%fused_computation.103 | loop fusion | flops 2605056 | bytes 2138128 | tf_op jit(solution)/shard_map/reduce_sum | solution.py:98
  154.5 35.4 %all-reduce.2.cloned.1.call-done = f32[8,16,384]{2,1,0:T(8,128)} async-done(((f32[8,16,384]{2,1,0:T(8,128)}), f32[8,16,384]{2,1,0:T(8,128)}) %all-reduce.2.cloned.1.call-update) | async-done | bytes 196624 | tf_op jit(solution)/shard_map/psum | solution.py:98
  189.8 1.6 broadcast_multiply_fusion
  (97 shorter events, 23.1 us)
Async XLA Ops:
  6.5 3.4 %copy-start = (f32[1,8,16,384]{3,2,1,0:T(8,128)S(1)}, f32[1,8,16,384]{3,2,1,0:T(8,128)}, u32[]{:S(2)}) copy-start(f32[1,8,16,384]{3,2,1,0:T(8,128)} %param.8) | copy-start | bytes 589828
  6.5 183.3 %all-reduce.2.cloned.1.call-start = ((), (), s32[]{:S(2)}) async-start(), calls=%async_computation | async-start | bytes 393216 | tf_op jit(solution)/shard_map/psum | solution.py:98
  7.4 45.7 %collective-permute-start = (f32[1,2,16,384]{3,2,1,0:T(8,128)S(1)}, f32[1,2,16,384]{3,2,1,0:T(8,128)S(1)}, u32[]{:S(2)}, u32[]{:S(2)}) collective-permute-start(f32[1,2,16,384]{3,2,1,0:T(8,128)S(1)} %get-tuple-element.40), channel_id=1, source_target_pairs={{0,8},{8,16},{16,24},{24,0},{1,9},{9,17},{17,25},{25,1},{2,10},{10... | collective-permute-start | bytes 147464 | tf_op jit(solution)/shard_map/ppermute | solution.py:19
  7.9 45.3 %collective-permute-start.1 = (f32[1,2,16,384]{3,2,1,0:T(8,128)S(1)}, f32[1,2,16,384]{3,2,1,0:T(8,128)S(1)}, u32[]{:S(2)}, u32[]{:S(2)}) collective-permute-start(f32[1,2,16,384]{3,2,1,0:T(8,128)S(1)} %get-tuple-element.39), channel_id=1, source_target_pairs={{8,0},{16,8},{24,16},{0,24},{9,1},{17,9},{25,17},{1,25},{10,2},{18... | collective-permute-start | bytes 147464 | tf_op jit(solution)/shard_map/ppermute | solution.py:22
  10.2 1.0 copy-start.2
  14.3 0.8 copy-start.4
  41.4 0.7 copy-start.3
  53.3 2.1 %copy-start.6 = (f32[4]{0:T(128)S(1)}, f32[4]{0:T(128)}, u32[]{:S(2)}) copy-start(f32[4]{0:T(128)} %param.13) | copy-start | bytes 52
  53.3 4.1 %collective-permute-start.2 = (f32[1,12,2,384]{3,2,1,0:T(2,128)S(1)}, f32[1,12,2,384]{3,2,1,0:T(2,128)S(1)}, u32[]{:S(2)}, u32[]{:S(2)}) collective-permute-start(f32[1,12,2,384]{3,2,1,0:T(2,128)S(1)} %get-tuple-element.14), channel_id=1, source_target_pairs={{0,4},{4,0},{1,5},{5,1},{2,6},{6,2},{3,7},{7,3},{8,12},{12,8},{9,1... | collective-permute-start | bytes 110600 | tf_op jit(solution)/shard_map/ppermute | solution.py:19
  53.8 4.4 %collective-permute-start.3 = (f32[1,12,2,384]{3,2,1,0:T(2,128)S(1)}, f32[1,12,2,384]{3,2,1,0:T(2,128)S(1)}, u32[]{:S(2)}, u32[]{:S(2)}) collective-permute-start(f32[1,12,2,384]{3,2,1,0:T(2,128)S(1)} %get-tuple-element.15), channel_id=1, source_target_pairs={{4,0},{0,4},{5,1},{1,5},{6,2},{2,6},{7,3},{3,7},{12,8},{8,12},{13,... | collective-permute-start | bytes 110600 | tf_op jit(solution)/shard_map/ppermute | solution.py:22
  56.1 2.6 %copy-start.1 = (f32[8,16,384]{2,1,0:T(8,128)S(1)}, f32[8,16,384]{2,1,0:T(8,128)}, u32[]{:S(2)}) copy-start(f32[8,16,384]{2,1,0:T(8,128)} %param.9) | copy-start | bytes 589828
  58.1 0.6 copy-start.5
  60.3 40.3 %collective-permute-start.4 = (f32[1,2,16,384]{3,2,1,0:T(8,128)S(1)}, f32[1,2,16,384]{3,2,1,0:T(8,128)S(1)}, u32[]{:S(2)}, u32[]{:S(2)}) collective-permute-start(f32[1,2,16,384]{3,2,1,0:T(8,128)S(1)} %get-tuple-element.34), channel_id=1, source_target_pairs={{0,8},{8,16},{16,24},{24,0},{1,9},{9,17},{17,25},{25,1},{2,10},{10... | collective-permute-start | bytes 147464 | tf_op jit(solution)/shard_map/ppermute | solution.py:19
  60.4 40.3 %collective-permute-start.5 = (f32[1,2,16,384]{3,2,1,0:T(8,128)S(1)}, f32[1,2,16,384]{3,2,1,0:T(8,128)S(1)}, u32[]{:S(2)}, u32[]{:S(2)}) collective-permute-start(f32[1,2,16,384]{3,2,1,0:T(8,128)S(1)} %get-tuple-element.35), channel_id=1, source_target_pairs={{8,0},{16,8},{24,16},{0,24},{9,1},{17,9},{25,17},{1,25},{10,2},{18... | collective-permute-start | bytes 147464 | tf_op jit(solution)/shard_map/ppermute | solution.py:22
  100.7 4.4 %collective-permute-start.6 = (f32[1,12,2,384]{3,2,1,0:T(2,128)S(1)}, f32[1,12,2,384]{3,2,1,0:T(2,128)S(1)}, u32[]{:S(2)}, u32[]{:S(2)}) collective-permute-start(f32[1,12,2,384]{3,2,1,0:T(2,128)S(1)} %get-tuple-element.12), channel_id=1, source_target_pairs={{0,4},{4,0},{1,5},{5,1},{2,6},{6,2},{3,7},{7,3},{8,12},{12,8},{9,1... | collective-permute-start | bytes 110600 | tf_op jit(solution)/shard_map/ppermute | solution.py:19
  101.1 4.4 %collective-permute-start.7 = (f32[1,12,2,384]{3,2,1,0:T(2,128)S(1)}, f32[1,12,2,384]{3,2,1,0:T(2,128)S(1)}, u32[]{:S(2)}, u32[]{:S(2)}) collective-permute-start(f32[1,12,2,384]{3,2,1,0:T(2,128)S(1)} %get-tuple-element.13), channel_id=1, source_target_pairs={{4,0},{0,4},{5,1},{1,5},{6,2},{2,6},{7,3},{3,7},{12,8},{8,12},{13,... | collective-permute-start | bytes 110600 | tf_op jit(solution)/shard_map/ppermute | solution.py:22
  106.2 40.5 %collective-permute-start.8 = (f32[1,2,16,384]{3,2,1,0:T(8,128)S(1)}, f32[1,2,16,384]{3,2,1,0:T(8,128)S(1)}, u32[]{:S(2)}, u32[]{:S(2)}) collective-permute-start(f32[1,2,16,384]{3,2,1,0:T(8,128)S(1)} %get-tuple-element.16), channel_id=1, source_target_pairs={{0,8},{8,16},{16,24},{24,0},{1,9},{9,17},{17,25},{25,1},{2,10},{10... | collective-permute-start | bytes 147464 | tf_op jit(solution)/shard_map/ppermute | solution.py:19
  106.3 40.4 %collective-permute-start.9 = (f32[1,2,16,384]{3,2,1,0:T(8,128)S(1)}, f32[1,2,16,384]{3,2,1,0:T(8,128)S(1)}, u32[]{:S(2)}, u32[]{:S(2)}) collective-permute-start(f32[1,2,16,384]{3,2,1,0:T(8,128)S(1)} %get-tuple-element.17), channel_id=1, source_target_pairs={{8,0},{16,8},{24,16},{0,24},{9,1},{17,9},{25,17},{1,25},{10,2},{18... | collective-permute-start | bytes 147464 | tf_op jit(solution)/shard_map/ppermute | solution.py:22
  146.8 4.3 %collective-permute-start.10 = (f32[1,12,2,384]{3,2,1,0:T(2,128)S(1)}, f32[1,12,2,384]{3,2,1,0:T(2,128)S(1)}, u32[]{:S(2)}, u32[]{:S(2)}) collective-permute-start(f32[1,12,2,384]{3,2,1,0:T(2,128)S(1)} %get-tuple-element.10), channel_id=1, source_target_pairs={{0,4},{4,0},{1,5},{5,1},{2,6},{6,2},{3,7},{7,3},{8,12},{12,8},{9,1... | collective-permute-start | bytes 110600 | tf_op jit(solution)/shard_map/ppermute | solution.py:19
  147.3 4.2 %collective-permute-start.11 = (f32[1,12,2,384]{3,2,1,0:T(2,128)S(1)}, f32[1,12,2,384]{3,2,1,0:T(2,128)S(1)}, u32[]{:S(2)}, u32[]{:S(2)}) collective-permute-start(f32[1,12,2,384]{3,2,1,0:T(2,128)S(1)} %get-tuple-element.11), channel_id=1, source_target_pairs={{4,0},{0,4},{5,1},{1,5},{6,2},{2,6},{7,3},{3,7},{12,8},{8,12},{13,... | collective-permute-start | bytes 110600 | tf_op jit(solution)/shard_map/ppermute | solution.py:22
Sparse Core Ops, SparseCore 0:
  154.6 35.2 all-reduce.1
